TPU v7x, 128 devices: a whole 4x4x4 slice. The times are simulated.
128 devices in a mesh: blk: 32 (over x, y_hi, z), grp: 4 (over y_lo, core).
Axes of the slice: x: 4, y: 4 (y_hi: 2, y_lo: 2; y = y_hi * 2 + y_lo), z: 4, core: 2. Of those that a mesh axis runs over, the one named last changes fastest.
Arguments:
- amplitudes: bfloat16 [1920, 1920], P('blk'), may hold values from -6 to 6
- hole_panel: bfloat16 [1920, 32, 1920], P(None, 'blk', 'grp'), may hold values from -0.375 to 0.375
- virt_fock: bfloat16 [1920, 1920], replicated, may hold values from -0.125 to 0.125
- irrep_sizes: int32 [8], replicated, may hold values from 1 to 480, 1920 in all
- pair_irreps: int32 [32], P('blk'), may hold values from 0 to 7
Outputs:
- dressed: bfloat16 [1920, 32, 1920], P('grp', 'blk')
Inputs may be any that keep to these rules, and one draw needn't show every extreme that they name: `irrep_sizes`: the 8 entries sum to 1920.
All inputs are finite; a program needn't handle non-finite values.
Results may differ from a plain program's by a relative error of at most 0.0049.
Values may be sent and summed in bfloat16 or wider, within the bound.
A program may use at most 128 MiB of HBM per device.

v0:
```python
import jax
import jax.numpy as jnp
from jax import lax
from jax.sharding import PartitionSpec as P


def irrep_of(positions, block_sizes):
    bounds = jnp.cumsum(block_sizes)[:-1]
    return jnp.sum((positions[:, None] >= bounds[None, :]).astype(jnp.int32), axis=1)


def local(amplitudes, hole_panel, virt_fock, irrep_sizes, pair_irreps):
    virtuals = amplitudes.shape[1]
    occ_local = hole_panel.shape[1]
    quarter = hole_panel.shape[2]
    col_start = lax.axis_index("grp") * quarter
    rows_irrep = irrep_of(jnp.arange(virtuals, dtype=jnp.int32), irrep_sizes)
    cols_irrep = irrep_of(col_start + jnp.arange(quarter, dtype=jnp.int32), irrep_sizes)
    allowed = (
        jnp.bitwise_xor(rows_irrep[:, None, None], cols_irrep[None, None, :])
        == pair_irreps[None, :, None]
    )
    masked = jnp.where(allowed, hole_panel, jnp.zeros((), jnp.bfloat16))
    flattened = masked.reshape(virtuals, occ_local * quarter)
    coupled = jnp.dot(
        lax.all_gather(amplitudes, "blk", axis=0, tiled=True),
        flattened,
        preferred_element_type=jnp.float32,
    ).astype(jnp.bfloat16)
    coupled = coupled.reshape(virtuals, occ_local, quarter)
    fock_rows = lax.dynamic_slice_in_dim(virt_fock, col_start, quarter, 0)
    summed = lax.psum_scatter(
        jnp.einsum("ajb,be->aje", coupled, fock_rows, preferred_element_type=jnp.float32),
        "grp",
        scatter_dimension=0,
        tiled=True,
    )
    return summed.astype(jnp.bfloat16)


def solution(mesh):
    in_specs = (P("blk", None), P(None, "blk", "grp"), P(), P(), P("blk"))
    out_specs = P("grp", "blk", None)
    return jax.shard_map(local, mesh=mesh, in_specs=in_specs, out_specs=out_specs, check_vma=False)
```

profile of v0, /device:TPU:1, one launch (start us, length us, event | category | flops | bytes accessed | tf_op | source)
XLA Modules:
  0.0 277.2 jit_solution(7345954068258640997)
XLA Ops:
  6.5 0.0 all-gather.3.cloned.1.call-start
  6.5 0.7 all-gather.3.cloned.1.call-update
  7.3 0.0 reduce-scatter.2.cloned.1.call-start
  8.0 0.8 reduce-window.4
  8.8 0.1 convert_reduce_fusion
  8.9 0.1 convert_reduce_fusion.1
  9.0 0.0 copy-start
  9.0 105.4 %all-gather.3.cloned.1.call-done = bf16[32,60,1920]{2,1,0:T(8,128)(2,1)} async-done(((bf16[1,60,1920]{2,1,0:T(8,128)(2,1)}), bf16[32,60,1920]{2,1,0:T(8,128)(2,1)}) %all-gather.3.cloned.1.call-update) | async-done | bytes 7372816 | tf_op jit(solution)/shard_map/all_gather | solution.py:26
  114.4 8.9 %reshape.72 = bf16[1920,1920]{1,0:T(8,128)(2,1)} reshape(bf16[32,60,1920]{2,1,0:T(8,128)(2,1)} %all-gather.3.cloned.1.call-done) | data formatting | bytes 14745600
  123.3 0.0 copy-done
  123.3 14.5 %convolution_bitcast_fusion = f32[1920,1,1920]{2,0,1:T(8,128)} fusion(bf16[1920,1920]{1,0:T(8,128)(2,1)} %param.7, s32[]{:T(128)S(6)} %select_n.8, bf16[1920,1920]{1,0:T(8,128)(2,1)} %reshape.72, bf16[1920,1,480]{0,2,1:T(8,128)(2,1)S(1)} %copy-done, s32[]{:T(128)} %bitcast.13, s32[480]{0:T(512)S(1)} %convert_reduce_fusion.1, s32[1920]{0:T(1024)S(1)} %convert_reduce_fusion), kind=kOutput, calls=%fused_computation | convolution fusion | flops 7081574400 | bytes 25814916 | tf_op jit(solution)/shard_map/ajb,be->aje/dot_general | solution.py:33
  137.8 0.0 reduce-scatter.2.cloned.1.call-update
  137.8 129.1 %reduce-scatter.2.cloned.1.call-done = f32[480,1,1920]{2,0,1:T(8,128)} async-done(((f32[1920,1,1920]{2,0,1:T(8,128)}), f32[480,1,1920]{2,0,1:T(8,128)}) %reduce-scatter.2.cloned.1.call-update) | async-done | bytes 3686416 | tf_op jit(solution)/shard_map/reduce_scatter | solution.py:32
  266.9 3.5 %convert_element_type.16 = bf16[480,1,1920]{2,0,1:T(8,128)(2,1)} convert(f32[480,1,1920]{2,0,1:T(8,128)} %reduce-scatter.2.cloned.1.call-done) | non-fusion elementwise | flops 921600 | bytes 5529600 | tf_op jit(solution)/shard_map/convert_element_type | solution.py:38
  (2 shorter events, 0.0 us)
Async XLA Ops:
  6.5 107.9 %all-gather.3.cloned.1.call-start = ((), (), s32[]{:S(2)}) async-start(), calls=%async_computation.2 | async-start | bytes 8110080 | tf_op jit(solution)/shard_map/all_gather | solution.py:26
  7.3 259.7 %reduce-scatter.2.cloned.1.call-start = ((), (), s32[]{:S(2)}) async-start(), calls=%async_computation.1 | async-start | bytes 18432000 | tf_op jit(solution)/shard_map/reduce_scatter | solution.py:32
  9.0 114.3 %copy-start = (bf16[1920,1,480]{0,2,1:T(8,128)(2,1)S(1)}, bf16[1920,1,480]{0,2,1:T(8,128)(2,1)}, u32[]{:S(2)}) copy-start(bf16[1920,1,480]{0,2,1:T(8,128)(2,1)} %param.6) | copy-start | bytes 5529604
Sparse Core Ops, SparseCore 0:
  10.3 104.0 all-gather.2
  137.9 128.9 reduce-scatter.1
where the time goes:
time: 278 us; the launch traced here: 277 us
  waiting for transfers between devices  235 us (85%)
  matrix products  14.5 us (5%)
  between operations  14.1 us (5%)
  local copies, waits for them, and re-layouts  8.89 us (3%)
  other arithmetic  4.48 us (2%)
    reduce_scatter x1, waiting for transfers between devices, local(): lax.psum_scatter(jnp.einsum('ajb,be->aje', coupled, fock_rows, preferred_...  129 us
    all_gather x1, waiting for transfers between devices, local(): lax.all_gather(amplitudes, 'blk', axis=0, tiled=True)  105 us
    dot_general x1, matrix products, local(): jnp.einsum('ajb,be->aje', coupled, fock_rows, preferred_element_type=jnp....  14.5 us
    unnamed x3, local copies, waits for them, and re-layouts  8.89 us
  transfers between devices with their start and end apart: 2, of which 2 were waited for; matrix products, arithmetic and copies ran while one was open for 0% of the time, Pallas kernels for 0%

commit v1 on v0

v1 whole, which is shorter than its diff:
```python
import jax
import jax.numpy as jnp
from jax import lax
from jax.sharding import PartitionSpec as P


def irrep_of(positions, block_sizes):
    bounds = jnp.cumsum(block_sizes)[:-1]
    return jnp.sum((positions[:, None] >= bounds[None, :]).astype(jnp.int32), axis=1)


def make_local(n_blk, n_grp):
    def local(amplitudes, hole_panel, virt_fock, irrep_sizes, pair_irreps):
        rows = amplitudes.shape[0]
        virtuals = amplitudes.shape[1]
        quarter = hole_panel.shape[2]
        g = lax.axis_index("grp")
        piece = rows // n_grp
        per = n_blk // n_grp
        perm = []
        for q in range(n_grp):
            for k in range(per):
                for i in range(n_grp):
                    perm.append(((per * q + k) * n_grp + i, (n_grp * k + i) * n_grp + q))
        mine = lax.dynamic_slice_in_dim(amplitudes, g * piece, piece, 0)
        mine = lax.ppermute(mine, ("blk", "grp"), perm)
        t_rows = lax.all_gather(mine, "blk", axis=0, tiled=True)
        labels = irrep_of(jnp.arange(virtuals, dtype=jnp.int32), irrep_sizes)
        panel = lax.all_gather(hole_panel.reshape(virtuals, quarter), "grp", axis=1, tiled=True)
        allowed = jnp.bitwise_xor(labels[:, None], labels[None, :]) == pair_irreps[0]
        masked = jnp.where(allowed, panel, jnp.zeros((), jnp.bfloat16))
        coupled = jnp.dot(t_rows, masked, preferred_element_type=jnp.float32).astype(jnp.bfloat16)
        out = jnp.dot(coupled, virt_fock, preferred_element_type=jnp.float32).astype(jnp.bfloat16)
        return out.reshape(quarter, 1, virtuals)

    return local


def solution(mesh):
    in_specs = (P("blk", None), P(None, "blk", "grp"), P(), P(), P("blk"))
    out_specs = P("grp", "blk", None)
    local = make_local(mesh.shape["blk"], mesh.shape["grp"])
    return jax.shard_map(local, mesh=mesh, in_specs=in_specs, out_specs=out_specs, check_vma=False)
```

time: 278 us -> 186 us (0.67)
  waiting for transfers between devices: 235 us -> 148 us
  local copies, waits for them, and re-layouts: 8.89 us -> 3.4 us
  starting transfers between devices: 0.04 us -> 4.98 us
  other arithmetic: 4.48 us -> 0.92 us
    reduce_scatter x1 -> x0, waiting for transfers between devices: 129 us -> none  [local(): lax.psum_scatter(jnp.einsum('ajb,be->aje', coupled, fock_rows, preferred_...]
    all_gather x1 -> x2, waiting for transfers between devices: 105 us -> 145 us  [the longest x1 73.9 us: local(): t_rows = lax.all_gather(mine, 'blk', axis=0, tiled=True)]
    unnamed x3 -> x5, local copies, waits for them, and re-layouts: 8.89 us -> 3.37 us
    ppermute x0 -> x1, starting transfers between devices: none -> 4.94 us  [local(): mine = lax.ppermute(mine, ('blk', 'grp'), perm)]
    convert_element_type x1 -> x0, other arithmetic: 3.46 us -> none  [local(): return summed.astype(jnp.bfloat16)]
  transfers between devices with their start and end apart: 2 -> 3, of which waited for: 2 -> 3; matrix products, arithmetic and copies ran while one was open for 0% -> 1% of each run, Pallas kernels for 0% -> 0%
where the time goes in v1:
time: 186 us
  waiting for transfers between devices  148 us (80%)
  matrix products  14.8 us (8%)
  between operations  14.1 us (8%)
  starting transfers between devices  4.98 us (3%)
  local copies, waits for them, and re-layouts  3.4 us (2%)
    all_gather x1, waiting for transfers between devices, local(): t_rows = lax.all_gather(mine, 'blk', axis=0, tiled=True)  73.9 us
    all_gather x1, waiting for transfers between devices, local(): lax.all_gather(hole_panel.reshape(virtuals, quarter), 'grp', axis=1, tile...  71.4 us
    dot_general x1, matrix products, local(): jnp.dot(coupled, virt_fock, preferred_element_type=jnp.float32)  14.8 us
    ppermute x1, starting transfers between devices, local(): mine = lax.ppermute(mine, ('blk', 'grp'), perm)  4.94 us
  transfers between devices with their start and end apart: 3, of which 3 were waited for; matrix products, arithmetic and copies ran while one was open for 1% of the time, Pallas kernels for 0%

profile of v1, /device:TPU:1, one launch (start us, length us, event | category | flops | bytes accessed | tf_op | source)
XLA Modules:
  0.0 186.1 jit_solution(730050720383567158)
XLA Ops:
  6.5 0.0 copy-start
  6.5 0.0 all-gather.7.cloned.1.call-start
  6.5 0.9 copy-done
  7.5 4.9 %collective-permute-start = (bf16[15,1920]{1,0:T(8,128)(2,1)S(1)}, bf16[15,1920]{1,0:T(8,128)(2,1)S(1)}, u32[]{:S(2)}, u32[]{:S(2)}) collective-permute-start(bf16[15,1920]{1,0:T(8,128)(2,1)S(1)} %constant_dynamic-slice_fusion), channel_id=1, source_target_pairs={{0,0},{1,4},{2,8},{3,12},{4,16},{5,20},{6,24},{7,28},{8,32},{9,36}... | collective-permute-start | bytes 172808 | tf_op jit(solution)/shard_map/ppermute | solution.py:26
  12.4 1.8 collective-permute-done
  14.3 0.0 copy-start.1
  14.3 0.6 copy-done.1
  14.9 0.0 all-gather.7.cloned.1.call-update
  14.9 0.0 all-gather.5.cloned.1.call-start
  14.9 0.7 all-gather.5.cloned.1.call-update
  15.7 0.8 reduce-window.4
  17.1 0.1 convert_reduce_fusion
  17.2 73.9 %all-gather.7.cloned.1.call-done = bf16[32,15,1920]{2,1,0:T(8,128)(2,1)} async-done(((bf16[1,15,1920]{2,1,0:T(8,128)(2,1)}), bf16[32,15,1920]{2,1,0:T(8,128)(2,1)}) %all-gather.7.cloned.1.call-update) | async-done | bytes 1843216 | tf_op jit(solution)/shard_map/all_gather | solution.py:27
  91.2 1.8 reshape.20
  93.0 71.4 %all-gather.5.cloned.1.call-done = bf16[1920,1,1920]{0,2,1:T(8,128)(2,1)} async-done(((bf16[1920,1,480]{0,2,1:T(8,128)(2,1)}), bf16[1920,1,1920]{0,2,1:T(8,128)(2,1)}) %all-gather.5.cloned.1.call-update) | async-done | bytes 7372816 | tf_op jit(solution)/shard_map/all_gather | solution.py:29
  164.4 14.8 %fusion.11 = bf16[480,1,1920]{2,0,1:T(8,128)(2,1)} fusion(bf16[1920,1920]{1,0:T(8,128)(2,1)} %param.7, bf16[480,1920]{1,0:T(8,128)(2,1)S(1)} %reshape.20, bf16[1920,1,1920]{0,2,1:T(8,128)(2,1)} %all-gather.5.cloned.1.call-done, s32[]{:T(128)} %bitcast.25, s32[1920]{0:T(1024)S(1)} %convert_reduce_fusion), kind=kOutput, calls=%fused_computation.10 | convolution fusion | flops 7090790400 | bytes 18439684 | tf_op jit(solution)/shard_map/dot_general | solution.py:33
  (2 shorter events, 0.0 us)
Async XLA Ops:
  6.5 0.9 copy-start
  6.5 84.6 %all-gather.7.cloned.1.call-start = ((), (), s32[]{:S(2)}) async-start(), calls=%async_computation.1 | async-start | bytes 2027520 | tf_op jit(solution)/shard_map/all_gather | solution.py:27
  7.5 6.7 %collective-permute-start = (bf16[15,1920]{1,0:T(8,128)(2,1)S(1)}, bf16[15,1920]{1,0:T(8,128)(2,1)S(1)}, u32[]{:S(2)}, u32[]{:S(2)}) collective-permute-start(bf16[15,1920]{1,0:T(8,128)(2,1)S(1)} %constant_dynamic-slice_fusion), channel_id=1, source_target_pairs={{0,0},{1,4},{2,8},{3,12},{4,16},{5,20},{6,24},{7,28},{8,32},{9,36}... | collective-permute-start | bytes 172808 | tf_op jit(solution)/shard_map/ppermute | solution.py:26
  14.3 0.6 copy-start.1
  14.9 149.5 %all-gather.5.cloned.1.call-start = ((), (), s32[]{:S(2)}) async-start(), calls=%async_computation | async-start | bytes 9216000 | tf_op jit(solution)/shard_map/all_gather | solution.py:29
Sparse Core Ops, SparseCore 0:
  15.0 76.1 all-gather.6
  92.8 71.5 all-gather.4

commit v2 on v1

v2 whole, which is shorter than its diff:
```python
import functools

import jax
import jax.numpy as jnp
from jax import lax
from jax.experimental import pallas as pl
from jax.experimental.pallas import tpu as pltpu
from jax.sharding import PartitionSpec as P

MESH = pl.DeviceIdType.MESH
F32, BF16 = jnp.float32, jnp.bfloat16
N = 1920
QR = 480
NB, NG = 32, 4
ROWS = 60
PAD = 64
WIN = 640
NT = N // 16
NW = (N - WIN) // 128 + 1
SPLIT = ((0, 512), (512, 512), (1024, 512), (1536, 384))
CH = 3
CR = QR // CH


def kernel(amp, wt, fock, sizes, pair, out,
           amp64, tbuf, cbuf, mfull, fbuf, coupled,
           scat_s, scat_r, ag_s, ag_r, pan_s, pan_r, f_sem):
    blk, g = lax.axis_index("blk"), lax.axis_index("grp")
    x, yh, z = blk // 8, (blk // 4) % 2, blk % 4
    yl, c = g // 2, g % 2

    def dev(x_, yh_, z_, yl_, c_):
        return (x_ * 8 + yh_ * 4 + z_, yl_ * 2 + c_)

    q = g
    d = (x - q + 4) % 4
    rel = d // 2
    src_c = (1 - rel) * ((c + 1 + d) % 2) + rel * (d - 2 + 2) % 2
    source = dev(q, (yh + rel) % 2, z, (yl + rel) % 2, src_c)
    tyl, tc = x // 2, x % 2
    trel = (yl + tyl) % 2
    td = (1 - trel) * (1 - (c + tc) % 2) + trel * (2 + c)
    target = dev((x + td) % 4, (yh + trel) % 2, z, tyl, tc)
    sibling = dev(x, yh, z, yl, 1 - c)
    other = dev(x, yh, z, 1 - yl, c)

    def plane(sx, sz):
        return dev((x + sx) % 4, yh, (z + sz) % 4, yl, c)

    bar = pltpu.get_barrier_semaphore()
    peers = [plane(s, 0) for s in (1, 2, 3)] + [plane(0, s) for s in (1, 2, 3)]
    for to in peers + [sibling, other, source]:
        pl.semaphore_signal(bar, inc=1, device_id=to, device_id_type=MESH)
    fcopy = pltpu.make_async_copy(fock, fbuf, f_sem)
    fcopy.start()
    amp64[pl.ds(0, ROWS), :] = amp[...]
    amp64[pl.ds(ROWS, PAD - ROWS), :] = jnp.zeros((PAD - ROWS, N), BF16)
    pl.semaphore_wait(bar, len(peers) + 3)

    pending = []

    th = ((td + 1) // 2) % 2
    for cl in range(2):
        col = pl.multiple_of(th * 896 + cl * 512, 128)
        copy = pltpu.make_async_remote_copy(
            amp64.at[:, pl.ds(col, 512)], tbuf.at[th * 2 + cl, yh * 4 + z],
            scat_s.at[cl], scat_r.at[cl], device_id=target, device_id_type=MESH)
        copy.start()
        pending.append(copy)

    p = pair[0]
    run = jnp.int32(0)
    bound = []
    for r in range(8):
        bound.append(run)
        run = run + sizes[r]
    bound.append(run)
    lo, hi, win = [], [], []
    for r in range(8):
        s = jnp.bitwise_xor(jnp.int32(r), p)
        first_lane, end_lane = jnp.int32(0), jnp.int32(0)
        for i in range(8):
            first_lane = jnp.where(s == i, bound[i], first_lane)
            end_lane = jnp.where(s == i, bound[i + 1], end_lane)
        lo.append(first_lane)
        hi.append(end_lane)
        win.append(jnp.minimum(jnp.right_shift(first_lane, 7), NW - 1))
    left_of = [lo[r] - win[r] * 128 for r in range(8)]
    right_of = [hi[r] - win[r] * 128 for r in range(8)]

    base = g * QR

    def pan_copy(kind, i, owner, to):
        rows = cbuf.at[pl.ds(pl.multiple_of(owner * QR + i * CR, 16), CR), :]
        return pltpu.make_async_remote_copy(
            rows, rows, pan_s.at[kind, i], pan_r.at[kind, i], device_id=to, device_id_type=MESH)

    lane = lax.broadcasted_iota(jnp.int32, (16, 128), 1)
    sub = lax.broadcasted_iota(jnp.int32, (16, 128), 0)

    def of_row(b, values):
        pick = jnp.full((16, 128), values[0])
        for r in range(1, 8):
            pick = jnp.where(b >= bound[r], values[r], pick)
        return pick

    def masks(b):
        w = of_row(b, win).astype(F32).astype(BF16)
        return [w == jnp.asarray(v, BF16) for v in range(NW)]

    def compact(t, _):
        row = pl.multiple_of(t * 16, 16)
        b = sub + (base + row)
        at = masks(b)
        left, right = of_row(b, left_of), of_row(b, right_of)
        for j in range(WIN // 128):
            acc = wt[pl.ds(row, 16), pl.ds(j * 128, 128)]
            for v in range(1, NW):
                acc = jnp.where(at[v], wt[pl.ds(row, 16), pl.ds((v + j) * 128, 128)], acc)
            keep = (lane + j * 128 >= left) & (lane + j * 128 < right)
            acc = jnp.where(keep, acc.astype(F32), 0.0).astype(BF16)
            cbuf[pl.ds(pl.multiple_of(base + row, 16), 16), pl.ds(j * 128, 128)] = acc
        return 0

    for i in range(CH):
        lax.fori_loop(i * (CR // 16), (i + 1) * (CR // 16), compact, 0)
        for kind, to in ((0, other), (1, sibling)):
            copy = pan_copy(kind, i, g, to)
            copy.start()
            pending.append(copy)

    def slot(dx, dz, cl):
        xo, zo = (x - dx + 4) % 4, (z - dz + 4) % 4
        do = (xo - q + 4) % 4
        return tbuf.at[(((do + 1) // 2) % 2) * 2 + cl, ((yh + do // 2) % 2) * 4 + zo]

    count = [0, 0]

    def axes(cl, a, b):
        return (a, b) if cl == 0 else (b, a)

    def send(cl, a, b, sa, sb):
        dx, dz = axes(cl, a, b)
        sx, sz = axes(cl, sa, sb)
        there = cl * 16 + ((a + sa) % 4) * 4 + (b + sb) % 4
        where = slot(dx, dz, cl)
        copy = pltpu.make_async_remote_copy(
            where, where, ag_s.at[cl * 16 + count[cl]], ag_r.at[there],
            device_id=plane(sx, sz), device_id_type=MESH)
        count[cl] += 1
        copy.start()
        pending.append(copy)

    def arrived(cl, a, b):
        dx, dz = axes(cl, a, b)
        where = slot(dx, dz, cl)
        pltpu.make_async_remote_copy(
            where, where, ag_s.at[cl * 16 + 15], ag_r.at[cl * 16 + a * 4 + b],
            device_id=sibling, device_id_type=MESH).wait_recv()

    for cl in range(2):
        where = slot(0, 0, cl)
        pltpu.make_async_remote_copy(
            where, where, scat_s.at[cl], scat_r.at[cl], device_id=sibling, device_id_type=MESH).wait_recv()
        for s in (1, 3, 2):
            send(cl, 0, 0, s, 0)
        send(cl, 0, 0, 0, 1)
        send(cl, 0, 0, 0, 3)
    for a in (1, 3, 2):
        for cl in range(2):
            arrived(cl, a, 0)
            send(cl, a, 0, 0, 1)
            send(cl, a, 0, 0, 3)
    for a, b in ((0, 1), (3, 3), (1, 1), (2, 3)):
        for cl in range(2):
            arrived(cl, a, b)
            send(cl, a, b, 0, b)

    for i in range(CH):
        pan_copy(0, i, (1 - yl) * 2 + c, sibling).wait_recv()
        copy = pan_copy(2, i, (1 - yl) * 2 + c, sibling)
        copy.start()
        pending.append(copy)
    for i in range(CH):
        pan_copy(1, i, yl * 2 + 1 - c, sibling).wait_recv()
        pan_copy(2, i, (1 - yl) * 2 + 1 - c, sibling).wait_recv()

    def expand(t, _):
        row = pl.multiple_of(t * 16, 16)
        at = masks(sub + row)
        part = [cbuf[pl.ds(row, 16), pl.ds(j * 128, 128)] for j in range(WIN // 128)]
        for k in range(N // 128):
            acc = jnp.zeros((16, 128), BF16)
            for j in range(WIN // 128):
                if 0 <= k - j < NW:
                    acc = jnp.where(at[k - j], part[j], acc)
            mfull[pl.ds(row, 16), pl.ds(k * 128, 128)] = acc
        return 0

    lax.fori_loop(0, NT, expand, 0)
    fcopy.wait()

    for cl in range(2):
        for a in range(4):
            for b in (1, 2, 3):
                if (a, b) not in ((0, 1), (3, 3), (1, 1), (2, 3)):
                    arrived(cl, a, b)
    for copy in pending:
        copy.wait_send()

    for col, width in SPLIT:
        acc = jnp.zeros((8 * PAD, width), F32)
        for ci, off, at in ((0, 0, 0), (1, 0, 512), (2, 128, 1024), (3, 0, 1408)):
            lhs = tbuf[ci].reshape(8 * PAD, 512)[:, off:]
            acc = acc + lax.dot_general(
                lhs, mfull[pl.ds(col, width), pl.ds(at, 512 - off)],
                (((1,), (1,)), ((), ())), preferred_element_type=F32)
        coupled[:, pl.ds(col, width)] = acc.astype(BF16)

    for col, width in SPLIT:
        acc = jnp.dot(coupled[...], fbuf[:, pl.ds(col, width)], preferred_element_type=F32)
        for k in range(8):
            out[pl.ds(k * ROWS, ROWS), pl.ds(col, width)] = acc[k * PAD:k * PAD + ROWS].astype(BF16)


def local(amplitudes, hole_panel, virt_fock, irrep_sizes, pair_irreps):
    wt = jnp.transpose(hole_panel.reshape(N, QR))
    vmem = pl.BlockSpec(memory_space=pltpu.VMEM)
    smem = pl.BlockSpec(memory_space=pltpu.SMEM)
    out = pl.pallas_call(
        kernel,
        out_shape=jax.ShapeDtypeStruct((QR, N), BF16),
        in_specs=[vmem, vmem, pl.BlockSpec(memory_space=pl.ANY), smem, smem],
        out_specs=vmem,
        scratch_shapes=[
            pltpu.VMEM((PAD, N), BF16),
            pltpu.VMEM((4, 8, PAD, 512), BF16),
            pltpu.VMEM((N, WIN), BF16),
            pltpu.VMEM((N, N), BF16),
            pltpu.VMEM((N, N), BF16),
            pltpu.VMEM((8 * PAD, N), BF16),
            pltpu.SemaphoreType.DMA((2,)),
            pltpu.SemaphoreType.DMA((2,)),
            pltpu.SemaphoreType.DMA((32,)),
            pltpu.SemaphoreType.DMA((32,)),
            pltpu.SemaphoreType.DMA((3, CH)),
            pltpu.SemaphoreType.DMA((3, CH)),
            pltpu.SemaphoreType.DMA,
        ],
        compiler_params=pltpu.CompilerParams(
            collective_id=0, has_side_effects=True, vmem_limit_bytes=50 << 20),
    )(amplitudes, wt, virt_fock, irrep_sizes, pair_irreps)
    return out.reshape(QR, 1, N)


def solution(mesh):
    in_specs = (P("blk", None), P(None, "blk", "grp"), P(), P(), P("blk"))
    out_specs = P("grp", "blk", None)
    return jax.shard_map(local, mesh=mesh, in_specs=in_specs, out_specs=out_specs, check_vma=False)
```

time: 186 us -> 43.4 us (0.23)
  waiting for transfers between devices: 148 us -> 0 us
  Pallas kernels: 0 us -> 37.6 us
  matrix products: 14.8 us -> 0 us
  between operations: 14.1 us -> 0.67 us
  starting transfers between devices: 4.98 us -> 0 us
    all_gather x2 -> x0, waiting for transfers between devices: 145 us -> none  [the longest x1 73.9 us: local(): t_rows = lax.all_gather(mine, 'blk', axis=0, tiled=True)]
    pallas_call x0 -> x1, Pallas kernels: none -> 37.6 us  [local(): pl.pallas_call(kernel, out_shape=jax.ShapeDtypeStruct((QR, N), BF16), in_...]
    dot_general x1 -> x0, matrix products: 14.8 us -> none  [local(): jnp.dot(coupled, virt_fock, preferred_element_type=jnp.float32)]
    ppermute x1 -> x0, starting transfers between devices: 4.94 us -> none  [local(): mine = lax.ppermute(mine, ('blk', 'grp'), perm)]
    unnamed x5 -> x7, local copies, waits for them, and re-layouts: 3.37 us -> 4.33 us
  transfers between devices with their start and end apart: 3 -> 0, of which waited for: 3 -> 0; matrix products, arithmetic and copies ran while one was open for 1% -> 0% of each run, Pallas kernels for 0% -> 0%
where the time goes in v2:
time: 43.4 us; the launch traced here: 42.6 us
  Pallas kernels  37.6 us (87%)
  local copies, waits for them, and re-layouts  4.33 us (10%)
  between operations  0.67 us (2%)
    pallas_call x1, Pallas kernels, local(): pl.pallas_call(kernel, out_shape=jax.ShapeDtypeStruct((QR, N), BF16), in_...  37.6 us
    unnamed x7, local copies, waits for them, and re-layouts  4.33 us

profile of v2, /device:TPU:1, one launch (start us, length us, event | category | flops | bytes accessed | tf_op | source)
XLA Modules:
  0.0 42.6 jit_solution(3543986033540592803)
XLA Ops:
  0.7 0.0 copy-start
  0.7 1.5 %copy-done = bf16[1920,1,480]{0,2,1:T(8,128)(2,1)S(1)} copy-done((bf16[1920,1,480]{0,2,1:T(8,128)(2,1)S(1)}, bf16[1920,1,480]{0,2,1:T(8,128)(2,1)}, u32[]{:S(2)}) %copy-start) | copy-done | bytes 1843224
  2.2 0.0 copy-start.1
  2.2 0.9 %copy-done.1 = bf16[60,1920]{1,0:T(8,128)(2,1)S(1)} copy-done((bf16[60,1920]{1,0:T(8,128)(2,1)S(1)}, bf16[60,1920]{1,0:T(8,128)(2,1)}, u32[]{:S(2)}) %copy-start.1) | copy-done | bytes 230424
  3.1 0.0 copy-start.2
  3.1 0.7 %copy-done.2 = s32[8]{0:T(128)S(1)} copy-done((s32[8]{0:T(128)S(1)}, s32[8]{0:T(128)}, u32[]{:S(2)}) %copy-start.2) | copy-done | bytes 56
  3.8 37.6 %shard_map.55 = bf16[480,1920]{1,0:T(8,128)(2,1)S(1)} custom-call(bf16[60,1920]{1,0:T(8,128)(2,1)S(1)} %copy-done.1, bf16[480,1920]{1,0:T(8,128)(2,1)S(1)} %bitcast.5, bf16[1920,1920]{1,0:T(8,128)(2,1)} %fock.1, s32[8]{0:T(128)S(1)} %copy-done.2, s32[1]{0:T(128)S(6)} %copy.7.pair), custom_call_target="tpu_custom_call" | custom-call | tf_op jit(solution)/shard_map/pallas_call | solution.py:230
  41.3 1.2 %copy.8 = bf16[480,1,1920]{2,0,1:T(8,128)(2,1)} copy(bf16[480,1,1920]{2,0,1:T(8,128)(2,1)S(1)} %bitcast.4) | data formatting | bytes 3686400
Async XLA Ops:
  0.7 1.5 %copy-start = (bf16[1920,1,480]{0,2,1:T(8,128)(2,1)S(1)}, bf16[1920,1,480]{0,2,1:T(8,128)(2,1)}, u32[]{:S(2)}) copy-start(bf16[1920,1,480]{0,2,1:T(8,128)(2,1)} %param.6) | copy-start | bytes 5529604
  2.2 0.9 %copy-start.1 = (bf16[60,1920]{1,0:T(8,128)(2,1)S(1)}, bf16[60,1920]{1,0:T(8,128)(2,1)}, u32[]{:S(2)}) copy-start(bf16[60,1920]{1,0:T(8,128)(2,1)} %amp.1) | copy-start | bytes 691204
  3.1 0.7 %copy-start.2 = (s32[8]{0:T(128)S(1)}, s32[8]{0:T(128)}, u32[]{:S(2)}) copy-start(s32[8]{0:T(128)} %sizes.1) | copy-start | bytes 100

commit v3 on v2

v3 whole, which is shorter than its diff:
```python
import functools

import jax
import jax.numpy as jnp
from jax import lax
from jax.experimental import pallas as pl
from jax.experimental.pallas import tpu as pltpu
from jax.sharding import PartitionSpec as P

MESH = pl.DeviceIdType.MESH
F32, BF16 = jnp.float32, jnp.bfloat16
N = 1920
QR = 480
NB, NG = 32, 4
ROWS = 60
PAD = 64
WIN = 640
NW = (N - WIN) // 128 + 1
FWIN = 496
NF = (WIN - FWIN) // 16 + 1
SPLIT = ((0, 512), (512, 512), (1024, 512), (1536, 384))
CC = 384
CH = 4


def kernel(amp, wt, fock, sizes, pair, out,
           amp64, tbuf, cbuf, ctb, cts, mfull, fall, coupled,
           a_s, a_r, b_s, b_r, pan_s, pan_r, f_sem):
    blk, g = lax.axis_index("blk"), lax.axis_index("grp")
    x, yh, z = blk // 8, (blk // 4) % 2, blk % 4
    yl, c = g // 2, g % 2

    def dev(x_, yh_, z_, yl_, c_):
        return (x_ * 8 + yh_ * 4 + z_, yl_ * 2 + c_)

    q = g
    d = (x - q + 4) % 4
    a_use = ((d + 3) % 4) // 2
    a_core = (a_use + c) % 2
    b_rel = d // 2
    b_core = (1 - b_rel) * ((c + 1 + d) % 2) + b_rel * ((d + 2) % 4)
    sources = [dev(q, yh, z, yl, a_core), dev(q, 1 - yh, z, 1 - yl, a_use),
               dev(q, (yh + b_rel) % 2, z, (yl + b_rel) % 2, b_core)]
    tyl, tc = x // 2, x % 2
    trel = (yl + tyl) % 2
    use = (1 - trel) * ((c + tc) % 2) + trel * c
    a_targets = [dev((x + 1 + 2 * use + i) % 4, (yh + trel) % 2, z, tyl, tc) for i in range(2)]
    td = (1 - trel) * (1 - (c + tc) % 2) + trel * (2 + c)
    b_target = dev((x + td) % 4, (yh + trel) % 2, z, tyl, tc)
    sibling = dev(x, yh, z, yl, 1 - c)
    other = dev(x, yh, z, 1 - yl, c)

    def plane(sx, sz):
        return dev((x + sx) % 4, yh, (z + sz) % 4, yl, c)

    bar = pltpu.get_barrier_semaphore()
    peers = [plane(s, 0) for s in (1, 2, 3)] + [plane(0, s) for s in (1, 2, 3)]
    for to in peers + sources + [sibling, other]:
        pl.semaphore_signal(bar, inc=1, device_id=to, device_id_type=MESH)
    far0 = (1 - yl) * 2
    fcopies = []
    for slot in range(4):
        owner = (yl * 2 + slot) % 4
        fcopies.append(pltpu.make_async_copy(
            fock.at[pl.ds(pl.multiple_of(owner * QR, 16), QR)],
            fall.at[pl.ds(slot * 512, QR)], f_sem.at[slot]))
    for copy in fcopies:
        copy.start()
    for slot in range(4):
        fall[pl.ds(slot * 512 + QR, 32), :] = jnp.zeros((32, N), BF16)
    amp64[pl.ds(0, ROWS), :] = amp[...]
    amp64[pl.ds(ROWS, PAD - ROWS), :] = jnp.zeros((PAD - ROWS, N), BF16)

    p = pair[0]
    run = jnp.int32(0)
    bound = []
    for r in range(8):
        bound.append(run)
        run = run + sizes[r]
    bound.append(run)
    lo, hi, win = [], [], []
    for r in range(8):
        s = jnp.bitwise_xor(jnp.int32(r), p)
        first_lane, end_lane = jnp.int32(0), jnp.int32(0)
        for i in range(8):
            first_lane = jnp.where(s == i, bound[i], first_lane)
            end_lane = jnp.where(s == i, bound[i + 1], end_lane)
        lo.append(first_lane)
        hi.append(end_lane)
        win.append(jnp.minimum(jnp.right_shift(first_lane, 7), NW - 1))
    fine = [jnp.minimum(jnp.right_shift(lo[r], 4), (N - FWIN) // 16) - win[r] * 8 for r in range(8)]
    left_of = [lo[r] - win[r] * 128 for r in range(8)]
    right_of = [hi[r] - win[r] * 128 for r in range(8)]

    base = g * QR

    def pan_copy(kind, i, owner, to):
        part = (ctb if kind == 1 else cts).at[owner, i]
        return pltpu.make_async_remote_copy(
            part, part, pan_s.at[kind, i], pan_r.at[kind, i], device_id=to, device_id_type=MESH)

    lane = lax.broadcasted_iota(jnp.int32, (16, 128), 1)
    sub = lax.broadcasted_iota(jnp.int32, (16, 128), 0)

    def of_row(b, values):
        pick = jnp.full((16, 128), values[0])
        for r in range(1, 8):
            pick = jnp.where(b >= bound[r], values[r], pick)
        return pick

    def masks(b):
        w = of_row(b, win).astype(F32).astype(BF16)
        return [w == jnp.asarray(v, BF16) for v in range(NW)]

    def compact(t, _):
        row = pl.multiple_of(t * 16, 16)
        b = sub + (base + row)
        at = masks(b)
        left, right = of_row(b, left_of), of_row(b, right_of)
        for j in range(WIN // 128):
            acc = wt[pl.ds(row, 16), pl.ds(j * 128, 128)]
            for v in range(1, NW):
                acc = jnp.where(at[v], wt[pl.ds(row, 16), pl.ds((v + j) * 128, 128)], acc)
            keep = (lane + j * 128 >= left) & (lane + j * 128 < right)
            acc = jnp.where(keep, acc.astype(F32), 0.0).astype(BF16)
            cbuf[pl.ds(row, 16), pl.ds(j * 128, 128)] = acc
        return 0

    lax.fori_loop(0, QR // 16, compact, 0)
    cbuf[pl.ds(QR, 32), :] = jnp.zeros((32, WIN), BF16)
    for i in range(CH):
        ctb[g, i] = jnp.transpose(cbuf[pl.ds(i * 128, 128), :])

    def fine_masks(owner, i):
        f = of_row(lane + (owner * QR + i * 128), fine).astype(F32).astype(BF16)
        return [f == jnp.asarray(v, BF16) for v in range(NF)]

    def narrow(i, _):
        at = fine_masks(g, i)
        for u in range(FWIN // 16):
            acc = ctb[g, i, pl.ds(u * 16, 16), :]
            for v in range(1, NF):
                acc = jnp.where(at[v], ctb[g, i, pl.ds((u + v) * 16, 16), :], acc)
            cts[g, i, pl.ds(u * 16, 16), :] = acc
        return 0

    def widen(owner, i):
        at = fine_masks(owner, i)
        for u in range(WIN // 16):
            acc = jnp.zeros((16, 128), BF16)
            for v in range(NF):
                if 0 <= u - v < FWIN // 16:
                    acc = jnp.where(at[v], cts[owner, i, pl.ds((u - v) * 16, 16), :], acc)
            ctb[owner, i, pl.ds(u * 16, 16), :] = acc

    lax.fori_loop(0, CH, narrow, 0)
    pl.semaphore_wait(bar, len(peers) + 5)

    pending = []

    def push(copy):
        copy.start()
        pending.append(copy)

    def columns(chunk):
        return pl.ds(pl.multiple_of(chunk * CC, 128), CC)

    def remote(src, dst, s_sem, r_sem, to):
        return pltpu.make_async_remote_copy(src, dst, s_sem, r_sem, device_id=to, device_id_type=MESH)

    mine = yh * 4 + z
    th = ((td + 1) // 2) % 2

    def a_first(s):
        for i in range(2):
            push(remote(amp64.at[:, columns(s)], tbuf.at[mine, :, columns(s)],
                        a_s.at[s * 2 + i], a_r.at[s, trel * 4],
                        a_targets[i]))

    def a_slot(e, dz, s):
        return tbuf.at[((yh + e) % 2) * 4 + (z - dz + 4) % 4, :, columns(s)]

    def a_send(e, dz, s, sz):
        where = a_slot(e, dz, s)
        n = 6 + s * 6 + (e * 2 + sz // 2 if dz == 0 else 4 + e)
        push(remote(where, where, a_s.at[n], a_r.at[s, e * 4 + (dz + sz) % 4], plane(0, sz)))

    def a_wait(e, dz, s):
        where = a_slot(e, dz, s)
        remote(where, where, a_s.at[0], a_r.at[s, e * 4 + dz], sibling).wait_recv()

    def b_slot(dx, dz):
        do = (x - dx - q + 8) % 4
        return tbuf.at[((yh + do // 2) % 2) * 4 + (z - dz + 4) % 4, :, columns(3 + ((do + 1) // 2) % 2)]

    def b_send(n, dx, dz, sx, sz):
        where = b_slot(dx, dz)
        push(remote(where, where, b_s.at[n], b_r.at[((dx + sx) % 4) * 4 + (dz + sz) % 4], plane(sx, sz)))

    def b_wait(dx, dz):
        where = b_slot(dx, dz)
        remote(where, where, b_s.at[0], b_r.at[dx * 4 + dz], sibling).wait_recv()

    push(remote(amp64.at[:, columns(3 + th)], tbuf.at[mine, :, columns(3 + th)],
                b_s.at[0], b_r.at[0], b_target))
    a_first(0)
    a_first(1)
    a_first(2)
    for i in range(CH):
        for kind, to in ((0, other), (1, sibling)):
            push(pan_copy(kind, i, g, to))

    def a_step(s):
        for e in range(2):
            a_wait(e, 0, s)
            a_send(e, 0, s, 1)
            a_send(e, 0, s, 3)

    def a_pass(s):
        a_wait(0, 1, s)
        a_send(0, 1, s, 1)
        a_wait(1, 3, s)
        a_send(1, 3, s, 3)

    def b_step(dz):
        if dz:
            b_wait(0, dz)
        b_send(4 + dz * 2, 0, dz, 1, 0)
        b_send(5 + dz * 2, 0, dz, 3, 0)

    def expand(owner, i, put):
        b = lane + (owner * QR + i * 128)
        w = of_row(b, win).astype(F32)
        w = jnp.where(lane + i * 128 < QR, w, -1.0).astype(BF16)
        at = [w == jnp.asarray(v, BF16) for v in range(NW)]

        def rows(u, _):
            row = pl.multiple_of(u * 16, 16)
            part = [ctb[owner, i, pl.ds(pl.multiple_of(j * 128 + row, 16), 16), :] for j in range(WIN // 128)]
            for k in range(N // 128):
                acc = jnp.zeros((16, 128), BF16)
                for j in range(WIN // 128):
                    if 0 <= k - j < NW:
                        acc = jnp.where(at[k - j], part[j], acc)
                put(pl.ds(pl.multiple_of(k * 128 + row, 16), 16), acc)
            return 0

        lax.fori_loop(0, 8, rows, 0)

    def expand_to(owner, slot, i):
        def put(rows, value):
            mfull[rows, pl.ds(pl.multiple_of(slot * 512 + i * 128, 128), 128)] = value
        expand(owner, i, put)

    def b_pass(dz, dx):
        b_wait(dx, dz)
        b_send(12 + dz, dx, dz, dx, 0)

    def pass_on(i):
        pan_copy(0, i, far0 + c, sibling).wait_recv()
        push(pan_copy(2, i, far0 + c, sibling))

    def far_ready(i):
        pan_copy(2, i, far0 + 1 - c, sibling).wait_recv()

    def b_pass(dz, dx):
        b_wait(dx, dz)
        b_send(12 + dz, dx, dz, dx, 0)

    def rows_of(at, width):
        return tbuf[:, :, pl.ds(at, width)].reshape(8 * PAD, width)

    def expand_own(owner, slot):
        def body(i, _):
            expand_to(owner, slot, i)
            return 0

        lax.fori_loop(0, CH, body, 0)

    def expand_far(lo, hi, owner, slot):
        def body(i, _):
            widen(owner, i)
            expand_to(owner, slot, i)
            return 0

        lax.fori_loop(lo, hi, body, 0)

    near, far, last = yl * 2 + 1 - c, far0 + c, far0 + 1 - c
    expand_own(g, c)
    b_wait(0, 0)
    for n, sz in ((1, 1), (2, 3), (3, 2)):
        b_send(n, 0, 0, 0, sz)
    b_step(0)
    a_step(0)
    a_step(1)
    b_step(1)
    b_step(3)
    for i in range(CH):
        pan_copy(1, i, near, sibling).wait_recv()
    expand_own(near, 1 - c)
    pass_on(0)
    b_step(2)
    a_step(2)
    a_pass(0)
    b_pass(0, 1)
    b_pass(3, 3)
    pass_on(1)
    expand_far(0, 2, far, 2 + c)
    b_pass(1, 1)
    b_pass(2, 3)
    pass_on(2)
    a_pass(1)
    a_pass(2)
    pass_on(3)
    expand_far(2, 4, far, 2 + c)
    for i in range(CH):
        far_ready(i)
    expand_far(0, 4, last, 3 - c)
    for copy in fcopies:
        copy.wait()
    for dx in (1, 2, 3):
        for dz in range(4):
            if (dz, dx) not in ((0, 1), (3, 3), (1, 1), (2, 3)):
                b_wait(dx, dz)
    for s in range(3):
        for e, dz in ((0, 2), (0, 3), (1, 1), (1, 2)):
            a_wait(e, dz, s)

    rows_t = tbuf[...].reshape(8 * PAD, N)
    for col in range(0, 2048, 512):
        coupled[:, pl.ds(col, 512)] = jnp.dot(
            rows_t, mfull[:, pl.ds(col, 512)], preferred_element_type=F32).astype(BF16)
    for col, width in SPLIT:
        acc = jnp.dot(coupled[...], fall[:, pl.ds(col, width)], preferred_element_type=F32)
        for k in range(8):
            out[pl.ds(k * ROWS, ROWS), pl.ds(col, width)] = acc[k * PAD:k * PAD + ROWS].astype(BF16)
    for copy in pending:
        copy.wait_send()


def local(amplitudes, hole_panel, virt_fock, irrep_sizes, pair_irreps):
    wt = jnp.transpose(hole_panel.reshape(N, QR))
    vmem = pl.BlockSpec(memory_space=pltpu.VMEM)
    smem = pl.BlockSpec(memory_space=pltpu.SMEM)
    out = pl.pallas_call(
        kernel,
        out_shape=jax.ShapeDtypeStruct((QR, N), BF16),
        in_specs=[vmem, vmem, pl.BlockSpec(memory_space=pl.ANY), smem, smem],
        out_specs=vmem,
        scratch_shapes=[
            pltpu.VMEM((PAD, N), BF16),
            pltpu.VMEM((8, PAD, N), BF16),
            pltpu.VMEM((512, WIN), BF16),
            pltpu.VMEM((NG, CH, WIN, 128), BF16),
            pltpu.VMEM((NG, CH, FWIN, 128), BF16),
            pltpu.VMEM((N, 2048), BF16),
            pltpu.VMEM((2048, N), BF16),
            pltpu.VMEM((8 * PAD, 2048), BF16),
            pltpu.SemaphoreType.DMA((24,)),
            pltpu.SemaphoreType.DMA((3, 8)),
            pltpu.SemaphoreType.DMA((16,)),
            pltpu.SemaphoreType.DMA((16,)),
            pltpu.SemaphoreType.DMA((3, CH)),
            pltpu.SemaphoreType.DMA((3, CH)),
            pltpu.SemaphoreType.DMA((4,)),
        ],
        compiler_params=pltpu.CompilerParams(
            collective_id=0, has_side_effects=True, vmem_limit_bytes=60 << 20),
    )(amplitudes, wt, virt_fock, irrep_sizes, pair_irreps)
    return out.reshape(QR, 1, N)


def solution(mesh):
    in_specs = (P("blk", None), P(None, "blk", "grp"), P(), P(), P("blk"))
    out_specs = P("grp", "blk", None)
    return jax.shard_map(local, mesh=mesh, in_specs=in_specs, out_specs=out_specs, check_vma=False)
```

time: 43.4 us -> 40.8 us (0.940); the launches traced: 42.6 us -> 40.6 us
  local copies, waits for them, and re-layouts: 4.33 us -> 2.87 us
  Pallas kernels: 37.6 us -> 37 us
    unnamed x7 -> x1, local copies, waits for them, and re-layouts: 4.33 us -> 2.87 us
    pallas_call x1, Pallas kernels: 37.6 us -> 37 us  [local(): pl.pallas_call(kernel, out_shape=jax.ShapeDtypeStruct((QR, N), BF16), in_...]
where the time goes in v3:
time: 40.8 us; the launch traced here: 40.6 us
  Pallas kernels  37 us (91%)
  local copies, waits for them, and re-layouts  2.87 us (7%)
  between operations  0.66 us (2%)
    pallas_call x1, Pallas kernels, local(): pl.pallas_call(kernel, out_shape=jax.ShapeDtypeStruct((QR, N), BF16), in_...  37 us
    unnamed x1, local copies, waits for them, and re-layouts  2.87 us

profile of v3, /device:TPU:1, one launch (start us, length us, event | category | flops | bytes accessed | tf_op | source)
XLA Modules:
  0.0 40.6 jit_solution(16822886045009367001)
XLA Ops:
  0.7 37.0 %shard_map.55 = bf16[480,1920]{1,0:T(8,128)(2,1)} custom-call(bf16[60,1920]{1,0:T(8,128)(2,1)} %amp.1, bf16[480,1920]{1,0:T(8,128)(2,1)} %bitcast.5, bf16[1920,1920]{1,0:T(8,128)(2,1)} %fock.1, s32[8]{0:T(128)} %sizes.1, s32[1]{0:T(128)S(6)} %copy.7.pair), custom_call_target="tpu_custom_call" | custom-call | tf_op jit(solution)/shard_map/pallas_call | solution.py:345
  37.7 2.9 %copy.8 = bf16[480,1,1920]{2,0,1:T(8,128)(2,1)} copy(bf16[480,1,1920]{2,0,1:T(8,128)(2,1)} %bitcast.4) | data formatting | bytes 3686400

commit v4 on v3

--- a/solution.py
+++ b/solution.py
@@ -18,13 +18,13 @@
 NW = (N - WIN) // 128 + 1
 FWIN = 496
 NF = (WIN - FWIN) // 16 + 1
-SPLIT = ((0, 512), (512, 512), (1024, 512), (1536, 384))
+SPLIT = ((0, 1024), (1024, 896))
 CC = 384
 CH = 4
 
 
 def kernel(amp, wt, fock, sizes, pair, out,
-           amp64, tbuf, cbuf, ctb, cts, mfull, fall, coupled,
+           amp64, tbuf, cbuf, ctb, cts, mfull, fall, rows_t, coupled,
            a_s, a_r, b_s, b_r, pan_s, pan_r, f_sem):
     blk, g = lax.axis_index("blk"), lax.axis_index("grp")
     x, yh, z = blk // 8, (blk // 4) % 2, blk % 4
@@ -95,7 +95,7 @@
     base = g * QR
 
     def pan_copy(kind, i, owner, to):
-        part = (ctb if kind == 1 else cts).at[owner, i]
+        part = (cts if kind == 0 else ctb).at[owner, i]
         return pltpu.make_async_remote_copy(
             part, part, pan_s.at[kind, i], pan_r.at[kind, i], device_id=to, device_id_type=MESH)
 
@@ -227,6 +227,7 @@
             b_wait(0, dz)
         b_send(4 + dz * 2, 0, dz, 1, 0)
         b_send(5 + dz * 2, 0, dz, 3, 0)
+        b_send(12 + dz, 0, dz, 2, 0)
 
     def expand(owner, i, put):
         b = lane + (owner * QR + i * 128)
@@ -252,41 +253,30 @@
             mfull[rows, pl.ds(pl.multiple_of(slot * 512 + i * 128, 128), 128)] = value
         expand(owner, i, put)
 
+    def pass_on(i):
+        pan_copy(0, i, far, sibling).wait_recv()
+        widen(far, i)
+        push(pan_copy(2, i, far, sibling))
+
+    def far_ready(i):
+        pan_copy(2, i, far0 + 1 - c, sibling).wait_recv()
+
     def b_pass(dz, dx):
         b_wait(dx, dz)
         b_send(12 + dz, dx, dz, dx, 0)
 
-    def pass_on(i):
-        pan_copy(0, i, far0 + c, sibling).wait_recv()
-        push(pan_copy(2, i, far0 + c, sibling))
-
-    def far_ready(i):
-        pan_copy(2, i, far0 + 1 - c, sibling).wait_recv()
-
-    def b_pass(dz, dx):
-        b_wait(dx, dz)
-        b_send(12 + dz, dx, dz, dx, 0)
-
     def rows_of(at, width):
         return tbuf[:, :, pl.ds(at, width)].reshape(8 * PAD, width)
 
-    def expand_own(owner, slot):
+    def expand_some(owner, slot, lo, hi):
         def body(i, _):
             expand_to(owner, slot, i)
             return 0
 
-        lax.fori_loop(0, CH, body, 0)
-
-    def expand_far(lo, hi, owner, slot):
-        def body(i, _):
-            widen(owner, i)
-            expand_to(owner, slot, i)
-            return 0
-
         lax.fori_loop(lo, hi, body, 0)
 
     near, far, last = yl * 2 + 1 - c, far0 + c, far0 + 1 - c
-    expand_own(g, c)
+    expand_some(g, c, 0, CH)
     b_wait(0, 0)
     for n, sz in ((1, 1), (2, 3), (3, 2)):
         b_send(n, 0, 0, 0, sz)
@@ -297,45 +287,40 @@
     b_step(3)
     for i in range(CH):
         pan_copy(1, i, near, sibling).wait_recv()
-    expand_own(near, 1 - c)
-    pass_on(0)
+    expand_some(near, 1 - c, 0, CH)
     b_step(2)
     a_step(2)
+    pass_on(0)
     a_pass(0)
-    b_pass(0, 1)
-    b_pass(3, 3)
     pass_on(1)
-    expand_far(0, 2, far, 2 + c)
-    b_pass(1, 1)
-    b_pass(2, 3)
+    expand_some(far, 2 + c, 0, 2)
+    a_pass(1)
     pass_on(2)
-    a_pass(1)
     a_pass(2)
     pass_on(3)
-    expand_far(2, 4, far, 2 + c)
+    expand_some(far, 2 + c, 2, CH)
     for i in range(CH):
         far_ready(i)
-    expand_far(0, 4, last, 3 - c)
+    expand_some(last, 3 - c, 0, CH)
     for copy in fcopies:
         copy.wait()
+    for copy in pending:
+        copy.wait_send()
     for dx in (1, 2, 3):
         for dz in range(4):
-            if (dz, dx) not in ((0, 1), (3, 3), (1, 1), (2, 3)):
-                b_wait(dx, dz)
+            b_wait(dx, dz)
     for s in range(3):
         for e, dz in ((0, 2), (0, 3), (1, 1), (1, 2)):
             a_wait(e, dz, s)
 
-    rows_t = tbuf[...].reshape(8 * PAD, N)
-    for col in range(0, 2048, 512):
-        coupled[:, pl.ds(col, 512)] = jnp.dot(
-            rows_t, mfull[:, pl.ds(col, 512)], preferred_element_type=F32).astype(BF16)
+    for k in range(8):
+        rows_t[pl.ds(k * ROWS, ROWS), :] = tbuf[k, pl.ds(0, ROWS), :]
+    for col in range(0, 2048, 1024):
+        coupled[:, pl.ds(col, 1024)] = jnp.dot(
+            rows_t[...], mfull[:, pl.ds(col, 1024)], preferred_element_type=F32).astype(BF16)
     for col, width in SPLIT:
-        acc = jnp.dot(coupled[...], fall[:, pl.ds(col, width)], preferred_element_type=F32)
-        for k in range(8):
-            out[pl.ds(k * ROWS, ROWS), pl.ds(col, width)] = acc[k * PAD:k * PAD + ROWS].astype(BF16)
-    for copy in pending:
-        copy.wait_send()
+        out[:, pl.ds(col, width)] = jnp.dot(
+            coupled[...], fall[:, pl.ds(col, width)], preferred_element_type=F32).astype(BF16)
 
 
 def local(amplitudes, hole_panel, virt_fock, irrep_sizes, pair_irreps):
@@ -355,7 +340,8 @@
             pltpu.VMEM((NG, CH, FWIN, 128), BF16),
             pltpu.VMEM((N, 2048), BF16),
             pltpu.VMEM((2048, N), BF16),
-            pltpu.VMEM((8 * PAD, 2048), BF16),
+            pltpu.VMEM((QR, N), BF16),
+            pltpu.VMEM((QR, 2048), BF16),
             pltpu.SemaphoreType.DMA((24,)),
             pltpu.SemaphoreType.DMA((3, 8)),
             pltpu.SemaphoreType.DMA((16,)),

time: 40.8 us -> 40.1 us (0.983); the launches traced: 40.6 us -> 39.4 us
  Pallas kernels: 37 us -> 35.9 us
    pallas_call x1, Pallas kernels: 37 us -> 35.9 us  [local(): pl.pallas_call(kernel, out_shape=jax.ShapeDtypeStruct((QR, N), BF16), in_...]
where the time goes in v4:
time: 40.1 us; the launch traced here: 39.4 us
  Pallas kernels  35.9 us (90%)
  local copies, waits for them, and re-layouts  2.87 us (7%)
  between operations  0.66 us (2%)
    pallas_call x1, Pallas kernels, local(): pl.pallas_call(kernel, out_shape=jax.ShapeDtypeStruct((QR, N), BF16), in_...  35.9 us
    unnamed x1, local copies, waits for them, and re-layouts  2.87 us

profile of v4, /device:TPU:1, one launch (start us, length us, event | category | flops | bytes accessed | tf_op | source)
XLA Modules:
  0.0 39.4 jit_solution(8670342572351479368)
XLA Ops:
  0.7 35.9 %shard_map.55 = bf16[480,1920]{1,0:T(8,128)(2,1)} custom-call(bf16[60,1920]{1,0:T(8,128)(2,1)} %amp.1, bf16[480,1920]{1,0:T(8,128)(2,1)} %bitcast.5, bf16[1920,1920]{1,0:T(8,128)(2,1)} %fock.1, s32[8]{0:T(128)} %sizes.1, s32[1]{0:T(128)S(6)} %copy.7.pair), custom_call_target="tpu_custom_call" | custom-call | tf_op jit(solution)/shard_map/pallas_call | solution.py:330
  36.5 2.9 %copy.8 = bf16[480,1,1920]{2,0,1:T(8,128)(2,1)} copy(bf16[480,1,1920]{2,0,1:T(8,128)(2,1)} %bitcast.4) | data formatting | bytes 3686400

commit v5 on v4

--- a/solution.py
+++ b/solution.py
@@ -309,12 +309,14 @@
     for dx in (1, 2, 3):
         for dz in range(4):
             b_wait(dx, dz)
+    for k in range(8):
+        rows_t[pl.ds(k * ROWS, ROWS), pl.ds(3 * CC, 2 * CC)] = tbuf[k, pl.ds(0, ROWS), pl.ds(3 * CC, 2 * CC)]
     for s in range(3):
         for e, dz in ((0, 2), (0, 3), (1, 1), (1, 2)):
             a_wait(e, dz, s)
 
     for k in range(8):
-        rows_t[pl.ds(k * ROWS, ROWS), :] = tbuf[k, pl.ds(0, ROWS), :]
+        rows_t[pl.ds(k * ROWS, ROWS), pl.ds(0, 3 * CC)] = tbuf[k, pl.ds(0, ROWS), pl.ds(0, 3 * CC)]
     for col in range(0, 2048, 1024):
         coupled[:, pl.ds(col, 1024)] = jnp.dot(
             rows_t[...], mfull[:, pl.ds(col, 1024)], preferred_element_type=F32).astype(BF16)

time: 40.1 us -> 40.1 us (level)
  no operation moved by 1% of the time
where the time goes in v5:
time: 40.1 us; the launch traced here: 39.4 us
  Pallas kernels  35.9 us (90%)
  local copies, waits for them, and re-layouts  2.87 us (7%)
  between operations  0.66 us (2%)
    pallas_call x1, Pallas kernels, local(): pl.pallas_call(kernel, out_shape=jax.ShapeDtypeStruct((QR, N), BF16), in_...  35.9 us
    unnamed x1, local copies, waits for them, and re-layouts  2.87 us

profile of v5, /device:TPU:1, one launch (start us, length us, event | category | flops | bytes accessed | tf_op | source)
XLA Modules:
  0.0 39.4 jit_solution(2224984481884773980)
XLA Ops:
  0.7 35.9 %shard_map.55 = bf16[480,1920]{1,0:T(8,128)(2,1)} custom-call(bf16[60,1920]{1,0:T(8,128)(2,1)} %amp.1, bf16[480,1920]{1,0:T(8,128)(2,1)} %bitcast.5, bf16[1920,1920]{1,0:T(8,128)(2,1)} %fock.1, s32[8]{0:T(128)} %sizes.1, s32[1]{0:T(128)S(6)} %copy.7.pair), custom_call_target="tpu_custom_call" | custom-call | tf_op jit(solution)/shard_map/pallas_call | solution.py:332
  36.6 2.9 %copy.8 = bf16[480,1,1920]{2,0,1:T(8,128)(2,1)} copy(bf16[480,1,1920]{2,0,1:T(8,128)(2,1)} %bitcast.4) | data formatting | bytes 3686400
